TPU v7x, 128 devices: a whole 4x4x4 slice. The times are simulated.
128 devices in a mesh: outer: 8 (over z, core), inner: 16 (over y, x).
Axes of the slice: x: 4, y: 4, z: 4, core: 2. Of those that a mesh axis runs over, the one named last changes fastest.
Arguments:
- tokens_in: bfloat16 [16384, 2048], P(('outer', 'inner')), may hold values from -6 to 6
- expert_ids: int32 [16384, 10], P(('outer', 'inner')), may hold values from 0 to 255, all different within a row; in each aligned block of 128 rows (0 to 127, 128 to 255, ...) at most 6 rows name the same one
- route_weight: float32 [16384, 10], P(('outer', 'inner')), may hold values from 0.05 to 1
- first_gain: float32 [2048], replicated, may hold values from 0.5 to 1.5
- gate_weight: bfloat16 [256, 2048, 512], P(('outer', 'inner')), may hold values from -0.125 to 0.125
- up_weight: bfloat16 [256, 2048, 512], P(('outer', 'inner')), may hold values from -0.125 to 0.125
- down_weight: bfloat16 [256, 512, 2048], P(('outer', 'inner')), may hold values from -0.25 to 0.25
- second_gain: float32 [2048], replicated, may hold values from 0.5 to 1.5
- mixer_weight: bfloat16 [2048, 4096], P(None, 'inner'), may hold values from -0.125 to 0.125
- gating_weight: bfloat16 [2048, 32], replicated, may hold values from -0.125 to 0.125
- filter_taps: bfloat16 [4, 4096], replicated, may hold values from -3 to 3
- decay_log: float32 [16], replicated, may hold values from -9 to -3
- decay_bias: float32 [16], replicated, may hold values from -1 to 1
- output_gain: float32 [128], replicated, may hold values from 0.5 to 1.5
Outputs:
- hidden_out: bfloat16 [16384, 2048], P(('outer', 'inner'))
- core_out: bfloat16 [16384, 2048], P(('outer', 'inner'))
Inputs may be any that keep to these rules, and one draw needn't show every extreme that they name: `expert_ids`: each token names 10 different experts; the 128 rows of one device name any one expert at most 6 times, a bound that some block reaches.
All inputs are finite; a program needn't handle non-finite values.
Results may differ from a plain program's by a relative error of at most 0.015.
Values may be sent and summed in bfloat16 or wider, within the bound.
A program may use at most 576 MiB of HBM per device.

v0:
```python
import jax
import jax.numpy as jnp
from jax import lax
from jax.sharding import PartitionSpec as P


def shifted(value, axis, steps):
    count = lax.axis_size(axis)
    leading, last = (max(0, -steps), min(count, count - steps))
    return lax.ppermute(value, axis, [(source, source + steps) for source in range(leading, last)])


def prefix_2(x, axis, join, neutral):
    place = lax.axis_index(axis)
    gathered = jax.tree.map(
        lambda a, kind: lax.all_gather(a.astype(kind), axis), x, (jnp.bfloat16, jnp.bfloat16)
    )
    state = jax.tree.map(lambda a, e: jnp.zeros_like(a) + jnp.asarray(e, a.dtype), x, neutral)

    def one(lap, state):
        return join(
            state,
            jax.tree.map(
                lambda a, own: lax.dynamic_index_in_dim(a, lap, 0, False).astype(own.dtype),
                gathered,
                x,
            ),
        )

    return lax.fori_loop(0, place, one, state)


def shortened(x):

    def short(part):
        return part.astype(jnp.bfloat16) if part.dtype == jnp.float32 else part

    return jax.tree.map(short, x)


def spread_2(value, axis, source):
    kept = jnp.where(lax.axis_index(axis) == source, value, 0).astype(value.dtype)
    return lax.psum(kept, axis)


def entering(x, axis, combine, identity):
    length, place = (lax.axis_size(axis), lax.axis_index(axis))
    everything = jax.tree.map(
        lambda part, kind: lax.all_gather(part.astype(kind), axis),
        x,
        jax.tree.map(lambda a: jnp.bfloat16 if a.dtype == jnp.float32 else a.dtype, x),
    )
    start = jax.tree.map(
        lambda part, zero: jnp.broadcast_to(jnp.asarray(zero, part.dtype), part.shape), x, identity
    )

    def lap(k, before):
        reached = k < place
        new = combine(
            before, jax.tree.map(lambda part, own: part[k].astype(own.dtype), everything, x)
        )
        return jax.tree.map(lambda a, b: jnp.where(reached, a, b), new, before)

    return lax.fori_loop(0, length, lap, start)


def rms_scale(values, gain):
    wide = values.astype(jnp.float32)
    return wide * lax.rsqrt(jnp.mean(wide * wide, axis=-1, keepdims=True) + 1e-06) * gain


def unit_heads(values):
    return values * lax.rsqrt(jnp.sum(values * values, axis=-1, keepdims=True) + 1e-06)


def run_experts(piece, gate_weight, up_weight, down_weight):
    gate = jnp.einsum("esd,edf->esf", piece, gate_weight, preferred_element_type=jnp.float32)
    upper = jnp.einsum("esd,edf->esf", piece, up_weight, preferred_element_type=jnp.float32)
    hidden = (jax.nn.silu(gate) * upper).astype(jnp.bfloat16)
    return jnp.einsum(
        "esf,efd->esd", hidden, down_weight, preferred_element_type=jnp.float32
    ).astype(jnp.bfloat16)


def unit_lower_inverse(system):
    size = system.shape[-1]
    if size == 1:
        return jnp.ones_like(system)
    half = size // 2
    both = unit_lower_inverse(jnp.stack([system[..., :half, :half], system[..., half:, half:]]))
    first, second = (both[0], both[1])
    corner = -jnp.einsum(
        "...ij,...jk->...ik",
        second,
        jnp.einsum(
            "...ij,...jk->...ik", system[..., half:, :half], first, precision=lax.Precision.HIGHEST
        ),
        precision=lax.Precision.HIGHEST,
    )
    top = jnp.concatenate([first, jnp.zeros_like(first)], axis=-1)
    bottom = jnp.concatenate([corner, second], axis=-1)
    return jnp.concatenate([top, bottom], axis=-2)


def join_maps(earlier, later):
    first_map, first_state = earlier
    next_map, next_state = later
    joined_map = jnp.einsum("hij,hjk->hik", next_map, first_map, precision=lax.Precision.HIGHEST)
    joined_state = (
        jnp.einsum("hij,hjv->hiv", next_map, first_state, precision=lax.Precision.HIGHEST)
        + next_state
    )
    return (joined_map, joined_state)


def per_device(
    tokens_in,
    expert_ids,
    route_weight,
    first_gain,
    gate_weight,
    up_weight,
    down_weight,
    second_gain,
    mixer_weight,
    gating_weight,
    filter_taps,
    decay_log,
    decay_bias,
    output_gain,
):
    n_outer = lax.axis_size("outer")
    n_inner = lax.axis_size("inner")
    n_dev = n_outer * n_inner
    tok_count, width = tokens_in.shape
    top_count = expert_ids.shape[1]
    local_experts = gate_weight.shape[0]
    experts_all = local_experts * n_dev
    capacity = max(2, 6 * tok_count * top_count // (5 * experts_all))
    normed_first = rms_scale(tokens_in, first_gain).astype(jnp.bfloat16)
    mix_weight = route_weight / jnp.sum(route_weight, axis=1, keepdims=True)
    flat_ids = expert_ids
    target = flat_ids % local_experts * (n_dev * capacity) + flat_ids // local_experts * capacity
    onehot = (
        flat_ids[:, :, None] == jnp.arange(experts_all, dtype=jnp.int32)[None, None, :]
    ).astype(jnp.int32)
    counted = jnp.sum(onehot, axis=1)
    before = jnp.cumsum(counted, axis=0) - counted
    slot_index = jnp.sum(before[:, None, :] * onehot, axis=2)
    target = target + slot_index
    slots = jnp.arange(n_dev * local_experts * capacity, dtype=jnp.int32)
    hits = target[:, :, None] == slots[None, None, :]
    dispatch = jnp.any(hits, axis=1).astype(jnp.bfloat16)
    outgoing = jnp.einsum(
        "ts,td->sd", dispatch, normed_first, preferred_element_type=jnp.float32
    ).astype(jnp.bfloat16)
    outgoing = outgoing.reshape(local_experts, n_dev * capacity, width)
    served = run_experts(
        lax.all_to_all(outgoing, ("outer", "inner"), split_axis=1, concat_axis=1, tiled=True),
        gate_weight,
        up_weight,
        down_weight,
    )
    returned = lax.all_to_all(served, ("outer", "inner"), split_axis=1, concat_axis=1, tiled=True)
    returned = returned.reshape(-1, width)
    combine = jnp.sum(jnp.where(hits, mix_weight[:, :, None], 0.0), axis=1)
    combine_hi = combine.astype(jnp.bfloat16)
    combine_lo = (combine - combine_hi.astype(jnp.float32)).astype(jnp.bfloat16)
    mixture = jnp.dot(combine_hi, returned, preferred_element_type=jnp.float32) + jnp.dot(
        combine_lo, returned, preferred_element_type=jnp.float32
    )
    hidden_out = (tokens_in.astype(jnp.float32) + mixture).astype(jnp.bfloat16)
    normed_second = rms_scale(hidden_out, second_gain).astype(jnp.bfloat16)
    mixed = jnp.dot(
        normed_second,
        lax.all_gather(mixer_weight, "inner", axis=1, tiled=True),
        preferred_element_type=jnp.float32,
    )
    projected = mixed.astype(jnp.bfloat16)
    gating = jnp.dot(normed_second, gating_weight, preferred_element_type=jnp.float32)
    taps = filter_taps.shape[0]
    rim = shifted(projected[tok_count - (taps - 1) :], ("outer", "inner"), 1)
    padded = jnp.concatenate([rim, projected], axis=0).astype(jnp.float32)
    filtered = jnp.zeros(projected.shape, jnp.float32)
    for tap_index in range(taps):
        filtered = (
            filtered
            + filter_taps[tap_index].astype(jnp.float32) * padded[tap_index : tap_index + tok_count]
        )
    filtered = jax.nn.silu(filtered)
    head_dim = output_gain.shape[0]
    value_heads = decay_log.shape[0]
    key_heads = (projected.shape[1] - value_heads * head_dim) // (2 * head_dim)
    ratio = value_heads // key_heads
    queries = unit_heads(
        filtered[:, : key_heads * head_dim].reshape(tok_count, key_heads, head_dim)
    ) * head_dim ** (-0.5)
    keys = unit_heads(
        filtered[:, key_heads * head_dim : 2 * key_heads * head_dim].reshape(
            tok_count, key_heads, head_dim
        )
    )
    values = filtered[:, 2 * key_heads * head_dim :].reshape(tok_count, value_heads, head_dim)
    queries = jnp.repeat(queries, ratio, axis=1)
    keys = jnp.repeat(keys, ratio, axis=1)
    strength = jax.nn.sigmoid(gating[:, :value_heads]).T
    log_decay = (-jnp.exp(decay_log) * jax.nn.softplus(gating[:, value_heads:] + decay_bias)).T
    cumulative = jnp.cumsum(log_decay, axis=1)
    positions = jnp.arange(tok_count)
    lower_incl = positions[:, None] >= positions[None, :]
    lower_strict = positions[:, None] > positions[None, :]
    spread = cumulative[:, :, None] - cumulative[:, None, :]
    decay_mat = jnp.where(lower_incl, jnp.exp(jnp.where(lower_incl, spread, 0.0)), 0.0)
    key_major = keys.transpose(1, 0, 2)
    query_leading = queries.transpose(1, 0, 2)
    value_major = values.transpose(1, 0, 2)
    key_inner = jnp.einsum("htd,hid->hti", key_major, key_major, precision=lax.Precision.HIGHEST)
    lower_part = jnp.where(lower_strict, decay_mat * key_inner, 0.0) * strength[:, :, None]
    system = lower_part + jnp.eye(tok_count, dtype=jnp.float32)
    growth = jnp.exp(cumulative)
    scaled_keys = key_major * (strength * growth)[:, :, None]
    scaled_values = value_major * strength[:, :, None]
    inverse = unit_lower_inverse(system)
    key_resolved = jnp.einsum("hts,hsd->htd", inverse, scaled_keys, precision=lax.Precision.HIGHEST)
    value_resolved = jnp.einsum(
        "hts,hsd->htd", inverse, scaled_values, precision=lax.Precision.HIGHEST
    )
    tail = jnp.exp(cumulative[:, -1:] - cumulative)
    trailing_keys = key_major * tail[:, :, None]
    eye_heads = jnp.broadcast_to(
        jnp.eye(head_dim, dtype=jnp.float32), (value_heads, head_dim, head_dim)
    )
    state_map = growth[:, -1][:, None, None] * eye_heads - jnp.einsum(
        "htk,htj->hkj", trailing_keys, key_resolved, precision=lax.Precision.HIGHEST
    )
    state_increment = jnp.einsum(
        "xbe,xbz->xez", trailing_keys, value_resolved, precision=lax.Precision.HIGHEST
    )
    identity = (eye_heads, jnp.zeros_like(state_increment))
    inner_pre = prefix_2((state_map, state_increment), "inner", join_maps, identity)
    inclusive = join_maps(inner_pre, (state_map, state_increment))
    group = spread_2(shortened(jnp.stack(inclusive)), "inner", n_inner - 1)
    outer_pre = entering((group[0], group[1]), "outer", join_maps, identity)
    prefix = join_maps(outer_pre, inner_pre)
    initial_state = prefix[1]
    updates = value_resolved - jnp.einsum(
        "mwx,mxd->mwd", key_resolved, initial_state, precision=lax.Precision.HIGHEST
    )
    query_key = (
        jnp.einsum("htd,hid->hti", query_leading, key_major, precision=lax.Precision.HIGHEST)
        * decay_mat
    )
    carried = (
        jnp.einsum("mwx,mxd->mwd", query_leading, initial_state, precision=lax.Precision.HIGHEST)
        * growth[:, :, None]
    )
    attended = carried + jnp.einsum(
        "hti,hiv->htv", query_key, updates, precision=lax.Precision.HIGHEST
    )
    attended = attended.transpose(1, 0, 2)
    core_out = (
        rms_scale(attended, output_gain)
        .astype(jnp.bfloat16)
        .reshape(tok_count, value_heads * head_dim)
    )
    return (hidden_out, core_out)


def solution(mesh):
    return jax.shard_map(
        per_device,
        mesh=mesh,
        in_specs=(
            P(("outer", "inner"), None),
            P(("outer", "inner"), None),
            P(("outer", "inner"), None),
            P(),
            P(("outer", "inner"), None, None),
            P(("outer", "inner"), None, None),
            P(("outer", "inner"), None, None),
            P(),
            P(None, "inner"),
            P(),
            P(),
            P(),
            P(),
            P(),
        ),
        out_specs=(P(("outer", "inner"), None), P(("outer", "inner"), None)),
        check_vma=False,
    )
```

profile of v0, /device:TPU:1, one launch (start us, length us, event | category | flops | bytes accessed | tf_op | source)
XLA Modules:
  0.0 724.9 jit_solution(11721711058515278131)
XLA Ops:
  13.5 2.9 convolution_convert_fusion
  16.4 13.0 %copy.112 = bf16[2,768,2048]{2,0,1:T(2,128)(2,1)S(1)} copy(bf16[2,768,2048]{2,1,0:T(8,128)(2,1)S(1)} %bitcast.186) | data formatting | bytes 12582912 | tf_op jit(solution)/shard_map/reshape | solution.py:157
  29.5 98.2 %all_to_all.10 = bf16[2,768,2048]{2,0,1:T(2,128)(2,1)S(1)} all-to-all(bf16[2,768,2048]{2,0,1:T(2,128)(2,1)S(1)} %copy.112), channel_id=1, replica_groups=mesh['outer'=8,'inner'=16] {'outer','inner'}, dimensions={1} | all-to-all | bytes 12582912 | tf_op jit(solution)/shard_map/all_to_all | solution.py:159
  130.3 5.3 fusion.18
  135.6 16.5 %convolution_convert_fusion.2 = bf16[2,768,2048]{2,1,0:T(8,128)(2,1)} fusion(bf16[2,512,2048]{2,1,0:T(8,128)(2,1)} %param.24, f32[2,768,512]{2,1,0:T(8,128)} %fusion.18, bf16[2,2048,512]{2,1,0:T(8,128)(2,1)} %param.23, bf16[2,768,2048]{2,0,1:T(2,128)(2,1)} %copy-done.12), kind=kOutput, calls=%fused_computation.26 | convolution fusion | flops 6450315264 | bytes 24117248 | tf_op jit(solution)/shard_map/esf,efd->esd/dot_general | solution.py:80
  152.1 12.7 %copy.115 = bf16[2,768,2048]{2,0,1:T(2,128)(2,1)} copy(bf16[2,768,2048]{2,1,0:T(8,128)(2,1)} %convolution_convert_fusion.2) | data formatting | bytes 12582912 | tf_op jit(solution)/shard_map/convert_element_type | solution.py:82
  164.8 12.8 %all-to-all-start.1 = ((bf16[2,768,2048]{2,0,1:T(2,128)(2,1)}), bf16[2,768,2048]{2,0,1:T(2,128)(2,1)}, u32[]{:S(2)}, u32[]{:S(2)}) async-start(bf16[2,768,2048]{2,0,1:T(2,128)(2,1)} %copy.115), calls=%async_computation.1 | async-start | bytes 12582912 | tf_op jit(solution)/shard_map/all_to_all | solution.py:164
  179.3 83.1 %all-to-all-done.1 = bf16[2,768,2048]{2,0,1:T(2,128)(2,1)} async-done(((bf16[2,768,2048]{2,0,1:T(2,128)(2,1)}), bf16[2,768,2048]{2,0,1:T(2,128)(2,1)}, u32[]{:S(2)}, u32[]{:S(2)}) %all-to-all-start.1) | async-done | bytes 6291488 | tf_op jit(solution)/shard_map/all_to_all | solution.py:164
  262.3 5.7 copy.116
  271.5 8.2 %convolution_convert_fusion.1 = bf16[128,4096]{1,0:T(8,128)(2,1)S(1)} fusion(bf16[2048,4096]{1,0:T(8,128)(2,1)} %all-gather.8.cloned.1.call-done, bf16[128,2048]{1,0:T(8,128)(2,1)S(1)} %get-tuple-element.227, f32[2048]{0:T(1024)S(1)} %copy-done.36, f32[128]{0:T(128)S(1)} %add_rsqrt_fusion.3), kind=kOutput, calls=%fused_computation.25 | convolution fusion | flops 2149056512 | bytes 18358784 | tf_op jit(solution)/shard_map/dot_general | solution.py:174
  279.7 9.9 %collective-permute-start = (bf16[3,4096]{1,0:T(4,128)(2,1)S(1)}, bf16[3,4096]{1,0:T(4,128)(2,1)S(1)}, u32[]{:S(2)}, u32[]{:S(2)}) collective-permute-start(bf16[3,4096]{1,0:T(4,128)(2,1)S(1)} %slice.199), channel_id=1, source_target_pairs={{0,1},{1,2},{2,3},{3,4},{4,5},{5,6},{6,7},{7,8},{8,9},{9,10},{10,1... | collective-permute-start | bytes 73736 | tf_op jit(solution)/shard_map/ppermute | solution.py:10
  307.1 4.7 fusion.111
  311.9 4.8 convolution_negate_fusion.5
  317.7 3.1 fusion.73
  333.3 3.0 fusion.119
  336.6 2.8 fusion.78
  339.3 2.8 fusion.118
  342.3 66.4 %all-gather.16.cloned.1.call-done = bf16[256,128,128]{2,1,0:T(8,128)(2,1)} async-done(((bf16[16,128,128]{2,1,0:T(8,128)(2,1)}), bf16[256,128,128]{2,1,0:T(8,128)(2,1)}) %all-gather.16.cloned.1.call-update) | async-done | bytes 8388624 | tf_op jit(solution)/shard_map/all_gather | solution.py:16
  408.6 72.5 %all-gather.14.cloned.1.call-done = bf16[256,128,128]{2,1,0:T(8,128)(2,1)} async-done(((bf16[16,128,128]{2,1,0:T(8,128)(2,1)}), bf16[256,128,128]{2,1,0:T(8,128)(2,1)}) %all-gather.14.cloned.1.call-update) | async-done | bytes 8388624 | tf_op jit(solution)/shard_map/all_gather | solution.py:16
  486.4 141.0 %all-reduce.9.cloned.1.call-done = bf16[2,16,128,128]{3,2,1,0:T(8,128)(2,1)} async-done(((bf16[2,16,128,128]{3,2,1,0:T(8,128)(2,1)}), bf16[2,16,128,128]{3,2,1,0:T(8,128)(2,1)}) %all-reduce.9.cloned.1.call-update) | async-done | bytes 1048592 | tf_op jit(solution)/shard_map/psum | solution.py:43
  632.0 3.3 convolution_multiply_fusion
  635.3 28.0 %all-gather.10.cloned.1.call-done = bf16[8,16,128,128]{3,2,1,0:T(8,128)(2,1)} async-done(((bf16[1,16,128,128]{3,2,1,0:T(8,128)(2,1)}), bf16[8,16,128,128]{3,2,1,0:T(8,128)(2,1)}) %all-gather.10.cloned.1.call-update) | async-done | bytes 4194320 | tf_op jit(solution)/shard_map/all_gather | solution.py:49
  663.3 33.7 %all-gather.12.cloned.1.call-done = bf16[8,16,128,128]{3,2,1,0:T(8,128)(2,1)} async-done(((bf16[1,16,128,128]{3,2,1,0:T(8,128)(2,1)}), bf16[8,16,128,128]{3,2,1,0:T(8,128)(2,1)}) %all-gather.12.cloned.1.call-update) | async-done | bytes 4194320 | tf_op jit(solution)/shard_map/all_gather | solution.py:49
  697.1 12.6 %while.27 = (s32[]{:T(128)}, bf16[16,128,128]{2,1,0:T(8,128)(2,1)S(1)}, s32[]{:T(128)}, bf16[8,16,128,128]{3,2,1,0:T(8,128)(2,1)}, bf16[8,16,128,128]{3,2,1,0:T(8,128)(2,1)}, /*index=5*/s32[]{:T(128)}, s32[]{:T(128)}) while((s32[]{:T(128)}, bf16[16,128,128]{2,1,0:T(8,128)(2,1)S(1)}, s32[]{:T(128)}, ...), condition=%wide.region_15.16_spmd.clone, body=%wide.region_14.15_spmd.clone.sunk | while | flops 68157440 | bytes 3672671 | solution.py:64
  (213 shorter events, 74.5 us)
Async XLA Ops:
  7.2 263.3 %copy-start = (bf16[2048,32]{0,1:T(8,128)(2,1)S(1)}, bf16[2048,32]{0,1:T(8,128)(2,1)}, u32[]{:S(2)}) copy-start(bf16[2048,32]{0,1:T(8,128)(2,1)} %param.27) | copy-start | bytes 393220
  7.2 264.3 %all-gather.8.cloned.1.call-start = ((), (), s32[]{:S(2)}) async-start(), calls=%async_computation.2 | async-start | bytes 17825792 | tf_op jit(solution)/shard_map/all_gather | solution.py:176
  29.4 100.8 %copy-start.44 = (bf16[2,2048,512]{2,1,0:T(8,128)(2,1)S(1)}, bf16[2,2048,512]{2,1,0:T(8,128)(2,1)}, u32[]{:S(2)}) copy-start(bf16[2,2048,512]{2,1,0:T(8,128)(2,1)} %param.22) | copy-start | bytes 12582916
  164.8 13.1 %copy-start.41 = (f32[128,10]{0,1:T(8,128)S(1)}, f32[128,10]{0,1:T(8,128)}, u32[]{:S(2)}) copy-start(f32[128,10]{0,1:T(8,128)} %param.20) | copy-start | bytes 15364
  164.8 13.2 %copy-start.45 = (f32[16]{0:T(128)S(1)}, f32[16]{0:T(128)}, u32[]{:S(2)}) copy-start(f32[16]{0:T(128)} %param.29) | copy-start | bytes 196
  164.8 14.4 %copy-start.35 = (bf16[4,4096]{1,0:T(4,128)(2,1)S(1)}, bf16[4,4096]{1,0:T(4,128)(2,1)}, u32[]{:S(2)}) copy-start(bf16[4,4096]{1,0:T(4,128)(2,1)} %param.28) | copy-start | bytes 98308
  164.8 97.5 %all-to-all-start.1 = ((bf16[2,768,2048]{2,0,1:T(2,128)(2,1)}), bf16[2,768,2048]{2,0,1:T(2,128)(2,1)}, u32[]{:S(2)}, u32[]{:S(2)}) async-start(bf16[2,768,2048]{2,0,1:T(2,128)(2,1)} %copy.115), calls=%async_computation.1 | async-start | bytes 12582912 | tf_op jit(solution)/shard_map/all_to_all | solution.py:164
  177.6 231.0 %all-gather.16.cloned.1.call-start = ((), (), s32[]{:S(2)}) async-start(), calls=%async_computation.7 | async-start | bytes 8912896 | tf_op jit(solution)/shard_map/all_gather | solution.py:16
  178.0 115.7 %copy-start.33 = (pred[128,128]{1,0:T(8,128)(4,1)}, pred[128,128]{1,0:T(8,128)(4,1)S(1)}, u32[]{:S(2)}) copy-start(pred[128,128]{1,0:T(8,128)(4,1)S(1)} %get-tuple-element.234) | copy-start | bytes 49156
  270.5 9.2 %copy-start.29 = (bf16[128,2048]{1,0:T(8,128)(2,1)}, bf16[128,2048]{1,0:T(8,128)(2,1)S(1)}, u32[]{:S(2)}) copy-start(bf16[128,2048]{1,0:T(8,128)(2,1)S(1)} %get-tuple-element.227) | copy-start | bytes 1572868
  279.7 10.6 %collective-permute-start = (bf16[3,4096]{1,0:T(4,128)(2,1)S(1)}, bf16[3,4096]{1,0:T(4,128)(2,1)S(1)}, u32[]{:S(2)}, u32[]{:S(2)}) collective-permute-start(bf16[3,4096]{1,0:T(4,128)(2,1)S(1)} %slice.199), channel_id=1, source_target_pairs={{0,1},{1,2},{2,3},{3,4},{4,5},{5,6},{6,7},{7,8},{8,9},{9,10},{10,1... | collective-permute-start | bytes 73736 | tf_op jit(solution)/shard_map/ppermute | solution.py:10
  297.6 19.1 %copy-start.26 = (f32[1,2,2,2,16,8,8]{6,5,4,3,2,1,0:T(8,128)}, f32[1,2,2,2,16,8,8]{6,5,4,3,2,1,0:T(8,128)S(1)}, u32[]{:S(2)}) copy-start(f32[1,2,2,2,16,8,8]{6,5,4,3,2,1,0:T(8,128)S(1)} %get-tuple-element.201) | copy-start | bytes 98308
  297.6 19.1 %copy-start.27 = (f32[1,2,2,2,16,8,8]{6,5,4,3,2,1,0:T(8,128)}, f32[1,2,2,2,16,8,8]{6,5,4,3,2,1,0:T(8,128)S(1)}, u32[]{:S(2)}) copy-start(f32[1,2,2,2,16,8,8]{6,5,4,3,2,1,0:T(8,128)S(1)} %get-tuple-element.202) | copy-start | bytes 98308
  307.1 9.5 %copy-start.30 = (f32[1,2,2,2,2,2,16,2,2]{8,7,6,5,4,3,2,1,0:T(2,128)S(1)}, f32[1,2,2,2,2,2,16,2,2]{8,7,6,5,4,3,2,1,0:T(2,128)}, u32[]{:S(2)}) copy-start(f32[1,2,2,2,2,2,16,2,2]{8,7,6,5,4,3,2,1,0:T(2,128)} %copy.134) | copy-start | bytes 24580
  307.1 9.5 %copy-start.31 = (f32[1,2,2,2,2,2,16,2,2]{8,7,6,5,4,3,2,1,0:T(2,128)S(1)}, f32[1,2,2,2,2,2,16,2,2]{8,7,6,5,4,3,2,1,0:T(2,128)}, u32[]{:S(2)}) copy-start(f32[1,2,2,2,2,2,16,2,2]{8,7,6,5,4,3,2,1,0:T(2,128)} %copy.135) | copy-start | bytes 24580
  329.7 6.6 copy-start.14
  329.7 6.6 copy-start.15
  333.3 8.9 %copy-start.6 = (f32[16,128,128]{2,1,0:T(8,128)}, f32[16,128,128]{2,1,0:T(8,128)S(1)}, u32[]{:S(2)}) copy-start(f32[16,128,128]{2,1,0:T(8,128)S(1)} %fusion.45) | copy-start | bytes 3145732
  336.3 144.8 %all-gather.14.cloned.1.call-start = ((), (), s32[]{:S(2)}) async-start(), calls=%async_computation.6 | async-start | bytes 8912896 | tf_op jit(solution)/shard_map/all_gather | solution.py:16
  342.2 285.2 %all-reduce.9.cloned.1.call-start = ((), (), s32[]{:S(2)}) async-start(), calls=%async_computation.3 | async-start | bytes 2097152 | tf_op jit(solution)/shard_map/psum | solution.py:43
  485.2 145.1 %copy-start.32 = (f32[16,8,8,128]{3,1,2,0:T(8,128)S(1)}, f32[16,8,8,128]{3,1,2,0:T(8,128)}, u32[]{:S(2)}) copy-start(f32[16,8,8,128]{3,1,2,0:T(8,128)} %get-tuple-element.186) | copy-start | bytes 1572868
  486.3 145.7 %copy-start.34 = (pred[128,128]{1,0:T(8,128)(4,1)S(1)}, pred[128,128]{1,0:T(8,128)(4,1)}, u32[]{:S(2)}) copy-start(pred[128,128]{1,0:T(8,128)(4,1)} %copy-done.33) | copy-start | bytes 49156
  486.3 177.0 %all-gather.10.cloned.1.call-start = ((), (), s32[]{:S(2)}) async-start(), calls=%async_computation.4 | async-start | bytes 4718592 | tf_op jit(solution)/shard_map/all_gather | solution.py:49
  629.7 67.4 %all-gather.12.cloned.1.call-start = ((), (), s32[]{:S(2)}) async-start(), calls=%async_computation.5 | async-start | bytes 4718592 | tf_op jit(solution)/shard_map/all_gather | solution.py:49
  (30 other events, 70.1 us)
Sparse Core Ops, SparseCore 0:
  10.1 225.6 all-gather.7
  336.4 72.1 all-gather.15
  410.8 70.3 all-gather.13
  486.4 140.9 all-reduce.8
  629.8 33.4 all-gather.9
  664.9 32.1 all-gather.11
where the time goes:
time: 731 us; the launch traced here: 725 us
  waiting for transfers between devices  426 us (58%)
  blocking collectives  98.2 us (13%)
  matrix products  93.1 us (13%)
  local copies, waits for them, and re-layouts  50 us (7%)
  starting transfers between devices  23.2 us (3%)
  other arithmetic  18.3 us (3%)
  between operations  15.7 us (2%)
    psum x1, waiting for transfers between devices, spread_2(): return lax.psum(kept, axis)  141 us
    all_gather x2, waiting for transfers between devices, prefix_2(): lax.all_gather(a.astype(kind), axis)  139 us
    all_to_all x1, blocking collectives, per_device(): lax.all_to_all(outgoing, ('outer', 'inner'), split_axis=1, concat_axis=1,...  98.2 us
    all_to_all x1, waiting for transfers between devices, per_device(): lax.all_to_all(served, ('outer', 'inner'), split_axis=1, concat_axis=1, t...  83.1 us
    all_gather x2, waiting for transfers between devices, entering(): lax.all_gather(part.astype(kind), axis)  61.7 us
    dot_general x1, matrix products, run_experts(): jnp.einsum('esf,efd->esd', hidden, down_weight, preferred_element_type=jn...  16.5 us
    dot_general x10, matrix products, join_maps(): jnp.einsum('hij,hjv->hiv', next_map, first_state, precision=lax.Precision...  15.1 us
  transfers between devices with their start and end apart: 8, of which 6 were waited for; matrix products, arithmetic and copies ran while one was open for 11% of the time, Pallas kernels for 0%

commit v1 on v0

--- a/solution.py
+++ b/solution.py
@@ -2,6 +2,12 @@
 import jax.numpy as jnp
 from jax import lax
 from jax.sharding import PartitionSpec as P
+from jax.lax import all_gather
+
+
+def expand_steps_all(w_in, along_axis):
+    met_up = jnp.sum(all_gather(w_in, axis_name=along_axis), 0)
+    return met_up
 
 
 def shifted(value, axis, steps):
@@ -40,7 +46,7 @@
 
 def spread_2(value, axis, source):
     kept = jnp.where(lax.axis_index(axis) == source, value, 0).astype(value.dtype)
-    return lax.psum(kept, axis)
+    return expand_steps_all(kept, axis)
 
 
 def entering(x, axis, combine, identity):

time: 731 us -> 763 us (1.044)
  waiting for transfers between devices: 426 us -> 449 us
  other arithmetic: 18.3 us -> 27.5 us
    all_gather x0 -> x1, waiting for transfers between devices: none -> 167 us  [expand_steps_all(): met_up = jnp.sum(all_gather(w_in, axis_name=along_axis), 0)]
    psum x1 -> x0, waiting for transfers between devices: 141 us -> none  [spread_2(): return lax.psum(kept, axis)]
    reduce_sum x0 -> x1, other arithmetic: none -> 9.28 us  [expand_steps_all(): met_up = jnp.sum(all_gather(w_in, axis_name=along_axis), 0)]
  transfers between devices with their start and end apart: 8 -> 8, of which waited for: 6 -> 6; matrix products, arithmetic and copies ran while one was open for 11% -> 10% of each run, Pallas kernels for 0% -> 0%
where the time goes in v1:
time: 763 us; the launch traced here: 757 us
  waiting for transfers between devices  449 us (59%)
  blocking collectives  98.2 us (13%)
  matrix products  93.1 us (12%)
  local copies, waits for them, and re-layouts  49.9 us (7%)
  other arithmetic  27.5 us (4%)
  starting transfers between devices  23.4 us (3%)
  between operations  15.7 us (2%)
    all_gather x1, waiting for transfers between devices, expand_steps_all(): met_up = jnp.sum(all_gather(w_in, axis_name=along_axis), 0)  167 us
    all_gather x2, waiting for transfers between devices, prefix_2(): lax.all_gather(a.astype(kind), axis)  138 us
    all_to_all x1, blocking collectives, per_device(): lax.all_to_all(outgoing, ('outer', 'inner'), split_axis=1, concat_axis=1,...  98.2 us
    all_to_all x1, waiting for transfers between devices, per_device(): lax.all_to_all(served, ('outer', 'inner'), split_axis=1, concat_axis=1, t...  83 us
    all_gather x2, waiting for transfers between devices, entering(): lax.all_gather(part.astype(kind), axis)  59.6 us
    dot_general x1, matrix products, run_experts(): jnp.einsum('esf,efd->esd', hidden, down_weight, preferred_element_type=jn...  16.6 us
  transfers between devices with their start and end apart: 8, of which 6 were waited for; matrix products, arithmetic and copies ran while one was open for 10% of the time, Pallas kernels for 0%

profile of v1, /device:TPU:1, one launch (start us, length us, event | category | flops | bytes accessed | tf_op | source)
XLA Modules:
  0.0 757.2 jit_solution(7710131618361502874)
XLA Ops:
  13.5 2.9 convolution_convert_fusion
  16.4 13.0 %copy.112 = bf16[2,768,2048]{2,0,1:T(2,128)(2,1)S(1)} copy(bf16[2,768,2048]{2,1,0:T(8,128)(2,1)S(1)} %bitcast.186) | data formatting | bytes 12582912 | tf_op jit(solution)/shard_map/reshape | solution.py:163
  29.5 98.2 %all_to_all.10 = bf16[2,768,2048]{2,0,1:T(2,128)(2,1)S(1)} all-to-all(bf16[2,768,2048]{2,0,1:T(2,128)(2,1)S(1)} %copy.112), channel_id=1, replica_groups=mesh['outer'=8,'inner'=16] {'outer','inner'}, dimensions={1} | all-to-all | bytes 12582912 | tf_op jit(solution)/shard_map/all_to_all | solution.py:165
  130.3 5.3 fusion.18
  135.6 16.6 %convolution_convert_fusion.2 = bf16[2,768,2048]{2,1,0:T(8,128)(2,1)} fusion(bf16[2,512,2048]{2,1,0:T(8,128)(2,1)} %param.24, f32[2,768,512]{2,1,0:T(8,128)} %fusion.18, bf16[2,2048,512]{2,1,0:T(8,128)(2,1)} %param.23, bf16[2,768,2048]{2,0,1:T(2,128)(2,1)} %copy-done.12), kind=kOutput, calls=%fused_computation.26 | convolution fusion | flops 6450315264 | bytes 24117248 | tf_op jit(solution)/shard_map/esf,efd->esd/dot_general | solution.py:86
  152.2 12.7 %copy.115 = bf16[2,768,2048]{2,0,1:T(2,128)(2,1)} copy(bf16[2,768,2048]{2,1,0:T(8,128)(2,1)} %convolution_convert_fusion.2) | data formatting | bytes 12582912 | tf_op jit(solution)/shard_map/convert_element_type | solution.py:88
  164.8 12.8 %all-to-all-start.1 = ((bf16[2,768,2048]{2,0,1:T(2,128)(2,1)}), bf16[2,768,2048]{2,0,1:T(2,128)(2,1)}, u32[]{:S(2)}, u32[]{:S(2)}) async-start(bf16[2,768,2048]{2,0,1:T(2,128)(2,1)} %copy.115), calls=%async_computation.1 | async-start | bytes 12582912 | tf_op jit(solution)/shard_map/all_to_all | solution.py:170
  179.3 83.0 %all-to-all-done.1 = bf16[2,768,2048]{2,0,1:T(2,128)(2,1)} async-done(((bf16[2,768,2048]{2,0,1:T(2,128)(2,1)}), bf16[2,768,2048]{2,0,1:T(2,128)(2,1)}, u32[]{:S(2)}, u32[]{:S(2)}) %all-to-all-start.1) | async-done | bytes 6291488 | tf_op jit(solution)/shard_map/all_to_all | solution.py:170
  262.3 5.7 copy.116
  271.4 8.2 %convolution_convert_fusion.1 = bf16[128,4096]{1,0:T(8,128)(2,1)S(1)} fusion(bf16[2048,4096]{1,0:T(8,128)(2,1)} %all-gather.9.cloned.1.call-done, bf16[128,2048]{1,0:T(8,128)(2,1)S(1)} %get-tuple-element.227, f32[2048]{0:T(1024)S(1)} %copy-done.35, f32[128]{0:T(128)S(1)} %add_rsqrt_fusion.3), kind=kOutput, calls=%fused_computation.25 | convolution fusion | flops 2149056512 | bytes 18358784 | tf_op jit(solution)/shard_map/dot_general | solution.py:180
  279.7 10.1 %collective-permute-start = (bf16[3,4096]{1,0:T(4,128)(2,1)S(1)}, bf16[3,4096]{1,0:T(4,128)(2,1)S(1)}, u32[]{:S(2)}, u32[]{:S(2)}) collective-permute-start(bf16[3,4096]{1,0:T(4,128)(2,1)S(1)} %slice.199), channel_id=1, source_target_pairs={{0,1},{1,2},{2,3},{3,4},{4,5},{5,6},{6,7},{7,8},{8,9},{9,10},{10,1... | collective-permute-start | bytes 73736 | tf_op jit(solution)/shard_map/ppermute | solution.py:16
  307.3 4.7 fusion.111
  312.1 4.8 convolution_negate_fusion.5
  317.8 3.1 fusion.73
  333.4 3.0 fusion.119
  339.5 2.8 fusion.118
  342.4 65.7 %all-gather.19.cloned.1.call-done = bf16[256,128,128]{2,1,0:T(8,128)(2,1)} async-done(((bf16[16,128,128]{2,1,0:T(8,128)(2,1)}), bf16[256,128,128]{2,1,0:T(8,128)(2,1)}) %all-gather.19.cloned.1.call-update) | async-done | bytes 8388624 | tf_op jit(solution)/shard_map/all_gather | solution.py:22
  408.1 72.5 %all-gather.17.cloned.1.call-done = bf16[256,128,128]{2,1,0:T(8,128)(2,1)} async-done(((bf16[16,128,128]{2,1,0:T(8,128)(2,1)}), bf16[256,128,128]{2,1,0:T(8,128)(2,1)}) %all-gather.17.cloned.1.call-update) | async-done | bytes 8388624 | tf_op jit(solution)/shard_map/all_gather | solution.py:22
  485.9 166.8 %all-gather.11.cloned.1.call-done = bf16[16,2,16,128,128]{4,3,2,1,0:T(8,128)(2,1)} async-done(((bf16[1,2,16,128,128]{4,3,2,1,0:T(8,128)(2,1)}), bf16[16,2,16,128,128]{4,3,2,1,0:T(8,128)(2,1)}) %all-gather.11.cloned.1.call-update) | async-done | bytes 16777232 | tf_op jit(solution)/shard_map/all_gather | solution.py:9
  652.7 9.3 %reduce_sum.101 = bf16[2,16,128,128]{3,2,1,0:T(8,128)(2,1)S(1)} reduce(bf16[16,2,16,128,128]{4,3,2,1,0:T(8,128)(2,1)} %all-gather.11.cloned.1.call-done, bf16[]{:T(256)} %constant.115.clone.1), dimensions={0}, to_apply=%region_13.14 | reduce | flops 7864320 | bytes 17825794 | tf_op jit(solution)/shard_map/reduce_sum | solution.py:9
  666.5 3.3 convolution_multiply_fusion
  669.8 25.9 %all-gather.13.cloned.1.call-done = bf16[8,16,128,128]{3,2,1,0:T(8,128)(2,1)} async-done(((bf16[1,16,128,128]{3,2,1,0:T(8,128)(2,1)}), bf16[8,16,128,128]{3,2,1,0:T(8,128)(2,1)}) %all-gather.13.cloned.1.call-update) | async-done | bytes 4194320 | tf_op jit(solution)/shard_map/all_gather | solution.py:55
  695.7 33.7 %all-gather.15.cloned.1.call-done = bf16[8,16,128,128]{3,2,1,0:T(8,128)(2,1)} async-done(((bf16[1,16,128,128]{3,2,1,0:T(8,128)(2,1)}), bf16[8,16,128,128]{3,2,1,0:T(8,128)(2,1)}) %all-gather.15.cloned.1.call-update) | async-done | bytes 4194320 | tf_op jit(solution)/shard_map/all_gather | solution.py:55
  729.4 12.6 %while.27 = (s32[]{:T(128)}, bf16[16,128,128]{2,1,0:T(8,128)(2,1)S(1)}, s32[]{:T(128)}, bf16[8,16,128,128]{3,2,1,0:T(8,128)(2,1)}, bf16[8,16,128,128]{3,2,1,0:T(8,128)(2,1)}, /*index=5*/s32[]{:T(128)}, s32[]{:T(128)}) while((s32[]{:T(128)}, bf16[16,128,128]{2,1,0:T(8,128)(2,1)S(1)}, s32[]{:T(128)}, ...), condition=%wide.region_15.16_spmd.clone, body=%wide.region_14.15_spmd.clone.sunk | while | flops 68157440 | bytes 3672671 | solution.py:70
  (212 shorter events, 77.1 us)
Async XLA Ops:
  7.2 263.3 %copy-start = (bf16[2048,32]{0,1:T(8,128)(2,1)S(1)}, bf16[2048,32]{0,1:T(8,128)(2,1)}, u32[]{:S(2)}) copy-start(bf16[2048,32]{0,1:T(8,128)(2,1)} %param.27) | copy-start | bytes 393220
  7.2 264.3 %all-gather.9.cloned.1.call-start = ((), (), s32[]{:S(2)}) async-start(), calls=%async_computation.2 | async-start | bytes 17825792 | tf_op jit(solution)/shard_map/all_gather | solution.py:182
  29.4 100.8 %copy-start.43 = (bf16[2,2048,512]{2,1,0:T(8,128)(2,1)S(1)}, bf16[2,2048,512]{2,1,0:T(8,128)(2,1)}, u32[]{:S(2)}) copy-start(bf16[2,2048,512]{2,1,0:T(8,128)(2,1)} %param.22) | copy-start | bytes 12582916
  164.8 13.1 %copy-start.40 = (f32[128,10]{0,1:T(8,128)S(1)}, f32[128,10]{0,1:T(8,128)}, u32[]{:S(2)}) copy-start(f32[128,10]{0,1:T(8,128)} %param.20) | copy-start | bytes 15364
  164.8 13.2 %copy-start.44 = (f32[16]{0:T(128)S(1)}, f32[16]{0:T(128)}, u32[]{:S(2)}) copy-start(f32[16]{0:T(128)} %param.29) | copy-start | bytes 196
  164.8 14.4 %copy-start.34 = (bf16[4,4096]{1,0:T(4,128)(2,1)S(1)}, bf16[4,4096]{1,0:T(4,128)(2,1)}, u32[]{:S(2)}) copy-start(bf16[4,4096]{1,0:T(4,128)(2,1)} %param.28) | copy-start | bytes 98308
  164.8 97.5 %all-to-all-start.1 = ((bf16[2,768,2048]{2,0,1:T(2,128)(2,1)}), bf16[2,768,2048]{2,0,1:T(2,128)(2,1)}, u32[]{:S(2)}, u32[]{:S(2)}) async-start(bf16[2,768,2048]{2,0,1:T(2,128)(2,1)} %copy.115), calls=%async_computation.1 | async-start | bytes 12582912 | tf_op jit(solution)/shard_map/all_to_all | solution.py:170
  177.6 230.5 %all-gather.19.cloned.1.call-start = ((), (), s32[]{:S(2)}) async-start(), calls=%async_computation.7 | async-start | bytes 8912896 | tf_op jit(solution)/shard_map/all_gather | solution.py:22
  178.0 115.9 %copy-start.32 = (pred[128,128]{1,0:T(8,128)(4,1)}, pred[128,128]{1,0:T(8,128)(4,1)S(1)}, u32[]{:S(2)}) copy-start(pred[128,128]{1,0:T(8,128)(4,1)S(1)} %get-tuple-element.234) | copy-start | bytes 49156
  270.5 9.2 %copy-start.29 = (bf16[128,2048]{1,0:T(8,128)(2,1)}, bf16[128,2048]{1,0:T(8,128)(2,1)S(1)}, u32[]{:S(2)}) copy-start(bf16[128,2048]{1,0:T(8,128)(2,1)S(1)} %get-tuple-element.227) | copy-start | bytes 1572868
  279.7 10.8 %collective-permute-start = (bf16[3,4096]{1,0:T(4,128)(2,1)S(1)}, bf16[3,4096]{1,0:T(4,128)(2,1)S(1)}, u32[]{:S(2)}, u32[]{:S(2)}) collective-permute-start(bf16[3,4096]{1,0:T(4,128)(2,1)S(1)} %slice.199), channel_id=1, source_target_pairs={{0,1},{1,2},{2,3},{3,4},{4,5},{5,6},{6,7},{7,8},{8,9},{9,10},{10,1... | collective-permute-start | bytes 73736 | tf_op jit(solution)/shard_map/ppermute | solution.py:16
  297.7 19.1 %copy-start.26 = (f32[1,2,2,2,16,8,8]{6,5,4,3,2,1,0:T(8,128)}, f32[1,2,2,2,16,8,8]{6,5,4,3,2,1,0:T(8,128)S(1)}, u32[]{:S(2)}) copy-start(f32[1,2,2,2,16,8,8]{6,5,4,3,2,1,0:T(8,128)S(1)} %get-tuple-element.201) | copy-start | bytes 98308
  297.8 19.1 %copy-start.27 = (f32[1,2,2,2,16,8,8]{6,5,4,3,2,1,0:T(8,128)}, f32[1,2,2,2,16,8,8]{6,5,4,3,2,1,0:T(8,128)S(1)}, u32[]{:S(2)}) copy-start(f32[1,2,2,2,16,8,8]{6,5,4,3,2,1,0:T(8,128)S(1)} %get-tuple-element.202) | copy-start | bytes 98308
  307.3 9.5 %copy-start.30 = (f32[1,2,2,2,2,2,16,2,2]{8,7,6,5,4,3,2,1,0:T(2,128)S(1)}, f32[1,2,2,2,2,2,16,2,2]{8,7,6,5,4,3,2,1,0:T(2,128)}, u32[]{:S(2)}) copy-start(f32[1,2,2,2,2,2,16,2,2]{8,7,6,5,4,3,2,1,0:T(2,128)} %copy.134) | copy-start | bytes 24580
  307.3 9.5 %copy-start.31 = (f32[1,2,2,2,2,2,16,2,2]{8,7,6,5,4,3,2,1,0:T(2,128)S(1)}, f32[1,2,2,2,2,2,16,2,2]{8,7,6,5,4,3,2,1,0:T(2,128)}, u32[]{:S(2)}) copy-start(f32[1,2,2,2,2,2,16,2,2]{8,7,6,5,4,3,2,1,0:T(2,128)} %copy.135) | copy-start | bytes 24580
  317.8 5.5 copy-start.23
  317.8 5.5 copy-start.25
  329.9 6.6 copy-start.14
  329.9 6.6 copy-start.15
  333.4 8.9 %copy-start.6 = (f32[16,128,128]{2,1,0:T(8,128)}, f32[16,128,128]{2,1,0:T(8,128)S(1)}, u32[]{:S(2)}) copy-start(f32[16,128,128]{2,1,0:T(8,128)S(1)} %fusion.45) | copy-start | bytes 3145732
  336.5 144.2 %all-gather.17.cloned.1.call-start = ((), (), s32[]{:S(2)}) async-start(), calls=%async_computation.6 | async-start | bytes 8912896 | tf_op jit(solution)/shard_map/all_gather | solution.py:22
  342.4 310.3 %all-gather.11.cloned.1.call-start = ((), (), s32[]{:S(2)}) async-start(), calls=%async_computation.3 | async-start | bytes 17825792 | tf_op jit(solution)/shard_map/all_gather | solution.py:9
  485.8 209.9 %all-gather.13.cloned.1.call-start = ((), (), s32[]{:S(2)}) async-start(), calls=%async_computation.4 | async-start | bytes 4718592 | tf_op jit(solution)/shard_map/all_gather | solution.py:55
  663.1 66.4 %all-gather.15.cloned.1.call-start = ((), (), s32[]{:S(2)}) async-start(), calls=%async_computation.5 | async-start | bytes 4718592 | tf_op jit(solution)/shard_map/all_gather | solution.py:55
  (29 other events, 64.8 us)
Sparse Core Ops, SparseCore 0:
  10.1 225.6 all-gather.8
  336.6 71.4 all-gather.18
  410.3 70.3 all-gather.16
  485.9 166.7 all-gather.10
  663.2 32.4 all-gather.12
  697.3 32.1 all-gather.14
